TPU v7x, 32 devices: a whole 2x2x4 slice. The times are simulated.
32 devices in a mesh: gx: 16 (over z, y, core), gy: 2 (over x).
Axes of the slice: x: 2, y: 2, z: 4, core: 2. Of those that a mesh axis runs over, the one named last changes fastest.
Arguments:
- positions: float32 [3, 65536], P(None, ('gx', 'gy')), may hold values from 0 to 6
- features: bfloat16 [64, 65536], P(None, ('gx', 'gy')), may hold values from -6 to 6
- halo_lists: int32 [2, 49152], P(None, ('gx', 'gy')), may hold values from 0 to 2047
- local_pairs: int32 [4, 196608], P(None, ('gx', 'gy')), may hold values from 0 to 2047, as said below
- cross_x: int32 [4, 65536], P(None, ('gx', 'gy')), may hold values from 0 to 2047, as said below
- cross_y: int32 [4, 65536], P(None, ('gx', 'gy')), may hold values from 0 to 2047, as said below
- pair_counts: int32 [32, 3], P(('gx', 'gy')), may hold values from 256 to 6144, as said below
- w_rbf: bfloat16 [8, 256], replicated, may hold values from -2 to 2
- w_src: bfloat16 [64, 256], replicated, may hold values from -0.75 to 0.75
- w_dst: bfloat16 [64, 256], replicated, may hold values from -0.75 to 0.75
- species_src: bfloat16 [4, 256], replicated, may hold values from -3 to 3
- species_dst: bfloat16 [4, 256], replicated, may hold values from -3 to 3
- w_hidden: bfloat16 [256, 256], replicated, may hold values from -0.375 to 0.375
- w_latent: bfloat16 [256, 64], replicated, may hold values from -0.375 to 0.375
- w_energy: float32 [64], replicated, may hold values from -0.75 to 0.75
Outputs:
- energy: float32 [1], replicated
- forces: float32 [3, 65536], P(None, ('gx', 'gy'))
- feature_grads: float32 [64, 65536], P(None, ('gx', 'gy'))
Inputs may be any that keep to these rules, and one draw needn't show every extreme that they name: `local_pairs`: rows 0 and 1 are different atoms of the block, below 2048; rows 2 and 3 are species below 4. `cross_x`: row 0 an atom below 2048, row 1 a slot below 1536, rows 2 and 3 species below 4. `cross_y`: row 0 an atom below 2048, row 1 a slot below 1536, rows 2 and 3 species below 4. `pair_counts`: column 0 counts live slots of local_pairs (at most 6144), columns 1 and 2 those of cross_x and cross_y (at most 2048); live slots come first; some device is full in each column.
All inputs are finite; a program needn't handle non-finite values.
Results may differ from a plain program's by a relative error of at most 0.0095.
Values may be sent and summed in bfloat16 or wider, within the bound.
No kernel may reach another device: no remote copies, remote signals or barrier semaphores. Data moves between devices by JAX's collectives and lax.ppermute only.
A program may use at most 64 MiB of HBM per device.

v0:
```python
import jax
import jax.numpy as jnp
from jax import lax
from jax.sharding import PartitionSpec as P

BLOCK = 512
cutoff_radius = 6.0
block_edge = 6.0
softening = 0.1


def shifted(array, axis, by):
    length = lax.axis_size(axis)
    return lax.ppermute(array, axis, [(i, (i + by) % length) for i in range(length)])


def pair_energy(
    src_pos, src_feat, dst_pos, dst_feat, spec_src, spec_dst, live_mask, offset, weights
):
    w_rbf, w_src, w_dst, species_src, species_dst, w_hidden, w_latent, w_energy = weights
    displace = dst_pos + offset[:, None] - src_pos
    radius = jnp.sqrt(jnp.sum(displace * displace, axis=0) + softening)
    orders = jnp.arange(1, w_rbf.shape[0] + 1).astype(jnp.float32)[:, None]
    basis = (jnp.sin(orders * (jnp.pi / cutoff_radius) * radius[None, :]) / radius[None, :]).astype(
        jnp.bfloat16
    )
    kinds = jnp.arange(species_src.shape[0], dtype=jnp.int32)[:, None]
    onehot_src = (spec_src[None, :] == kinds).astype(jnp.bfloat16)
    onehot_dst = (spec_dst[None, :] == kinds).astype(jnp.bfloat16)
    pre = jnp.dot(w_rbf.T, basis, preferred_element_type=jnp.float32)
    pre = pre + jnp.dot(w_src.T, src_feat.astype(jnp.bfloat16), preferred_element_type=jnp.float32)
    pre = pre + jnp.dot(w_dst.T, dst_feat.astype(jnp.bfloat16), preferred_element_type=jnp.float32)
    pre = pre + jnp.dot(species_src.T, onehot_src, preferred_element_type=jnp.float32)
    pre = pre + jnp.dot(species_dst.T, onehot_dst, preferred_element_type=jnp.float32)
    hidden = jax.nn.silu(pre).astype(jnp.bfloat16)
    second = jax.nn.silu(jnp.dot(w_hidden.T, hidden, preferred_element_type=jnp.float32)).astype(
        jnp.bfloat16
    )
    latent = jnp.dot(w_latent.T, second, preferred_element_type=jnp.float32)
    ratio = jnp.minimum(radius / cutoff_radius, 1.0)
    envelope = (1.0 - ratio**2) ** 2
    scores = jnp.dot(w_energy, latent, precision=lax.Precision.HIGHEST)
    return jnp.sum(envelope * scores * live_mask)


def block_grads(
    src_pos, src_feat, dst_pos, dst_feat, spec_src, spec_dst, live_mask, offset, weights
):

    def energy_of(pos_one, feat_one, pos_two, feat_two):
        return pair_energy(
            pos_one, feat_one, pos_two, feat_two, spec_src, spec_dst, live_mask, offset, weights
        )

    energy, pullback = jax.vjp(
        energy_of, src_pos, src_feat.astype(jnp.float32), dst_pos, dst_feat.astype(jnp.float32)
    )
    return (energy, pullback(jnp.ones_like(energy)))


def run_edges(
    src_pos, src_feat, dst_pos, dst_feat, spec_src, spec_dst, live_mask, live_count, offset, weights
):
    inputs = (src_pos, src_feat, dst_pos, dst_feat, spec_src, spec_dst, live_mask)
    edges = src_pos.shape[1]
    filled = (live_count + BLOCK - 1) // BLOCK
    start_grads = (
        jnp.zeros((3, edges), jnp.float32),
        jnp.zeros((src_feat.shape[0], edges), jnp.float32),
        jnp.zeros((3, edges), jnp.float32),
        jnp.zeros((dst_feat.shape[0], edges), jnp.float32),
    )

    def visit_live(index, carry):
        total, grads = carry
        begin = index * BLOCK
        blocks = tuple(
            (lax.dynamic_slice_in_dim(item, begin, BLOCK, axis=item.ndim - 1) for item in inputs)
        )
        energy, parts = block_grads(*blocks, offset, weights)
        grads = tuple(
            (
                lax.dynamic_update_slice_in_dim(whole, piece, begin, axis=1)
                for whole, piece in zip(grads, parts)
            )
        )
        return (total + energy, grads)

    return lax.fori_loop(0, filled, visit_live, (jnp.zeros((), jnp.float32), start_grads))


def on_device(
    positions,
    features,
    halo_lists,
    local_pairs,
    cross_x,
    cross_y,
    pair_counts,
    w_rbf,
    w_src,
    w_dst,
    species_src,
    species_dst,
    w_hidden,
    w_latent,
    w_energy,
):
    weights = (w_rbf, w_src, w_dst, species_src, species_dst, w_hidden, w_latent, w_energy)
    atoms = positions.shape[1]
    halo_size = halo_lists.shape[1]
    width = features.shape[0]
    list_x = halo_lists[0]
    list_y = halo_lists[1]
    got_pos_x = shifted(positions[:, list_x], "gx", -1)
    got_feat_x = shifted(features[:, list_x], "gx", -1)
    got_pos_y = shifted(positions[:, list_y], "gy", -1)
    got_feat_y = shifted(features[:, list_y], "gy", -1)
    zero_off = jnp.zeros((3,), jnp.float32)
    off_x = jnp.array([block_edge, 0.0, 0.0], jnp.float32)
    off_y = jnp.array([0.0, block_edge, 0.0], jnp.float32)
    counts = pair_counts[0]
    slots_loc = jnp.arange(local_pairs.shape[1], dtype=jnp.int32)
    slots_cross = jnp.arange(cross_x.shape[1], dtype=jnp.int32)
    live_loc = (slots_loc < counts[0]).astype(jnp.float32)
    flag_x = (slots_cross < counts[1]).astype(jnp.int32)
    flag_y = (slots_cross < counts[2]).astype(jnp.int32)
    source, target = (local_pairs[0], local_pairs[1])
    energy_loc, grads = run_edges(
        positions[:, source],
        features[:, source],
        positions[:, target],
        features[:, target],
        local_pairs[2],
        local_pairs[3],
        live_loc,
        counts[0],
        zero_off,
        weights,
    )
    grad_pos = (
        jnp.zeros((3, atoms), jnp.float32).at[:, source].add(grads[0]).at[:, target].add(grads[2])
    )
    grad_feat = (
        jnp.zeros((width, atoms), jnp.float32)
        .at[:, source]
        .add(grads[1])
        .at[:, target]
        .add(grads[3])
    )
    source_x, slot_x = (cross_x[0], cross_x[1])
    src_pos_x = positions[:, source_x]
    src_feat_x = features[:, source_x]
    energy_x, grads_x = run_edges(
        src_pos_x,
        src_feat_x,
        got_pos_x[:, slot_x],
        got_feat_x[:, slot_x],
        cross_x[2],
        cross_x[3],
        flag_x.astype(jnp.float32),
        counts[1],
        off_x,
        weights,
    )
    grad_pos = grad_pos.at[:, source_x].add(grads_x[0])
    grad_feat = grad_feat.at[:, source_x].add(grads_x[1])
    source_y, slot_y = (cross_y[0], cross_y[1])
    src_pos_y = positions[:, source_y]
    src_feat_y = features[:, source_y]
    energy_y, grads_y = run_edges(
        src_pos_y,
        src_feat_y,
        got_pos_y[:, slot_y],
        got_feat_y[:, slot_y],
        cross_y[2],
        cross_y[3],
        flag_y.astype(jnp.float32),
        counts[2],
        off_y,
        weights,
    )
    grad_pos = grad_pos.at[:, source_y].add(grads_y[0])
    grad_feat = grad_feat.at[:, source_y].add(grads_y[1])
    lent_pos_x = jnp.zeros((3, halo_size), jnp.float32).at[:, slot_x].add(grads_x[2])
    lent_feat_x = jnp.zeros((width, halo_size), jnp.float32).at[:, slot_x].add(grads_x[3])
    back_pos_x, back_feat_x = shifted((lent_pos_x, lent_feat_x), "gx", 1)
    lent_pos_y = jnp.zeros((3, halo_size), jnp.float32).at[:, slot_y].add(grads_y[2])
    lent_feat_y = jnp.zeros((width, halo_size), jnp.float32).at[:, slot_y].add(grads_y[3])
    back_pos_y, back_feat_y = shifted((lent_pos_y, lent_feat_y), "gy", 1)
    grad_pos = grad_pos.at[:, list_x].add(back_pos_x).at[:, list_y].add(back_pos_y)
    grad_feat = grad_feat.at[:, list_x].add(back_feat_x).at[:, list_y].add(back_feat_y)
    total = lax.psum(energy_loc + energy_x + energy_y, ("gx", "gy"))
    atoms_all = atoms * lax.axis_size("gx") * lax.axis_size("gy")
    energy = (total / atoms_all).reshape(1)
    return (energy, -grad_pos, grad_feat)


def solution(mesh):
    return jax.shard_map(
        on_device,
        mesh=mesh,
        in_specs=(
            P(None, ("gx", "gy")),
            P(None, ("gx", "gy")),
            P(None, ("gx", "gy")),
            P(None, ("gx", "gy")),
            P(None, ("gx", "gy")),
            P(None, ("gx", "gy")),
            P(("gx", "gy"), None),
            P(),
            P(),
            P(),
            P(),
            P(),
            P(),
            P(),
            P(),
        ),
        out_specs=(P(), P(None, ("gx", "gy")), P(None, ("gx", "gy"))),
        check_vma=False,
    )
```

profile of v0, /device:TPU:0, one launch (start us, length us, event | category | flops | bytes accessed | tf_op | source)
XLA Modules:
  0.0 767.4 jit_solution(1176307451014661208)
XLA Ops:
  31.0 20.9 %gather_fusion.1 = f32[6144,3]{1,0:T(8,128)} fusion(f32[3,2048]{0,1:T(8,128)S(1)} %copy.112, s32[6144]{0:T(1024)S(1)} %broadcast_clamp_fusion), kind=kCustom, calls=%fused_computation.1 | custom fusion | bytes 172032 | tf_op jit(solution)/shard_map/gather | solution.py:130
  51.9 22.1 %gather_fusion.2 = bf16[6144,64]{1,0:T(8,128)(2,1)} fusion(bf16[64,2048]{0,1:T(8,128)(2,1)S(1)} %copy.114, s32[6144]{0:T(1024)S(1)} %broadcast_clamp_fusion), kind=kCustom, calls=%fused_computation.2 | custom fusion | bytes 1597440 | tf_op jit(solution)/shard_map/gather | solution.py:131
  74.0 20.9 %gather_fusion = f32[6144,3]{1,0:T(8,128)} fusion(f32[3,2048]{0,1:T(8,128)S(1)} %copy.112, s32[6144]{0:T(1024)S(1)} %broadcast_clamp_fusion.1), kind=kCustom, calls=%fused_computation | custom fusion | bytes 172032 | tf_op jit(solution)/shard_map/gather | solution.py:132
  94.9 22.0 %gather_fusion.3 = bf16[6144,64]{1,0:T(8,128)(2,1)} fusion(bf16[64,2048]{0,1:T(8,128)(2,1)S(1)} %copy.114, s32[6144]{0:T(1024)S(1)} %broadcast_clamp_fusion.1), kind=kCustom, calls=%fused_computation.3 | custom fusion | bytes 1597440 | tf_op jit(solution)/shard_map/gather | solution.py:133
  185.6 17.9 %while.57 = (s32[]{:T(128)}, f32[]{:T(128)}, f32[3,2048]{1,0:T(4,128)S(1)}, f32[64,2048]{1,0:T(8,128)S(1)}, f32[3,2048]{1,0:T(4,128)S(1)}, /*index=5*/f32[64,204...) while((s32[]{:T(128)}, f32[]{:T(128)}, ...), condition=%wide.region_11.12_spmd.clone, body=%wide.region_6.11_spmd.sunk.clone.sunk | while | flops 246594080 | bytes 9612223 | solution.py:89
  210.1 20.8 %while.58 = (s32[]{:T(128)}, f32[]{:T(128)}, f32[3,2048]{1,0:T(4,128)S(1)}, f32[64,2048]{1,0:T(8,128)S(1)}, f32[3,2048]{1,0:T(4,128)S(1)}, /*index=5*/f32[64,204...) while((s32[]{:T(128)}, f32[]{:T(128)}, ...), condition=%wide.region_17.18_spmd.clone, body=%wide.region_12.17_spmd.sunk.clone.sunk | while | flops 246594080 | bytes 9743323 | solution.py:89
  232.2 12.0 %scatter_custom_fusion.12 = f32[64,1536]{0,1:T(8,128)S(1)} fusion(s32[2048]{0:T(1024)} %bitcast.415, f32[2048,64]{1,0:T(8,128)} %copy.162, f32[]{:T(128)} %constant.142.clone.1), kind=kCustom, calls=%fused_computation.275 | custom fusion | flops 131072 | bytes 393728 | tf_op jit(solution)/shard_map/scatter-add | solution.py:186
  245.3 10.9 %collective-permute-start.6 = (f32[64,1536]{1,0:T(8,128)}, f32[64,1536]{1,0:T(8,128)}, u32[]{:S(2)}, u32[]{:S(2)}) collective-permute-start(f32[64,1536]{1,0:T(8,128)} %copy.163), channel_id=1, source_target_pairs={{0,2},{2,4},{4,6},{6,8},{8,10},{10,12},{12,14},{14,16},{16,18},{18... | collective-permute-start | bytes 1179656 | tf_op jit(solution)/shard_map/ppermute | solution.py:14
  256.5 11.8 %scatter_custom_fusion.14 = f32[64,1536]{0,1:T(8,128)S(1)} fusion(s32[2048]{0:T(1024)} %bitcast.412, f32[2048,64]{1,0:T(8,128)S(1)} %copy.165, f32[]{:T(128)} %constant.142.clone.1), kind=kCustom, calls=%fused_computation.273 | custom fusion | flops 131072 | bytes 393728 | tf_op jit(solution)/shard_map/scatter-add | solution.py:189
  269.7 11.8 %scatter_custom_fusion.4 = f32[3,1536]{0,1:T(8,128)S(1)} fusion(s32[2048]{0:T(1024)} %bitcast.416, f32[2048,3]{1,0:T(8,128)S(1)} %copy.152, f32[]{:T(128)} %constant.142.clone.1), kind=kCustom, calls=%fused_computation.279 | custom fusion | flops 6144 | bytes 18944 | tf_op jit(solution)/shard_map/scatter-add | solution.py:185
  282.4 26.4 %collective-permute-start.4 = (f32[3,1536]{1,0:T(4,128)}, f32[3,1536]{1,0:T(4,128)}, u32[]{:S(2)}, u32[]{:S(2)}) collective-permute-start(f32[3,1536]{1,0:T(4,128)} %copy.153), channel_id=1, source_target_pairs={{0,2},{2,4},{4,6},{6,8},{8,10},{10,12},{12,14},{14,16},{16,18},{18... | collective-permute-start | bytes 55304 | tf_op jit(solution)/shard_map/ppermute | solution.py:14
  309.1 11.8 %scatter_custom_fusion.6 = f32[3,1536]{0,1:T(8,128)S(1)} fusion(s32[2048]{0:T(1024)} %bitcast.413, f32[2048,3]{1,0:T(8,128)S(1)} %copy.155, f32[]{:T(128)} %constant.142.clone.1), kind=kCustom, calls=%fused_computation.277 | custom fusion | flops 6144 | bytes 18944 | tf_op jit(solution)/shard_map/scatter-add | solution.py:188
  323.5 40.1 %while.56 = (s32[]{:T(128)}, f32[]{:T(128)}, f32[3,6144]{1,0:T(4,128)S(1)}, f32[64,6144]{1,0:T(8,128)S(1)}, f32[3,6144]{1,0:T(4,128)S(1)}, /*index=5*/f32[64,614...) while((s32[]{:T(128)}, f32[]{:T(128)}, ...), condition=%wide.region_5.6_spmd, body=%wide.region_0.5_spmd.sunk | while | flops 246594080 | bytes 9610155 | solution.py:89
  372.5 33.7 %scatter_custom_fusion.8 = f32[64,2048]{0,1:T(8,128)S(1)} fusion(s32[6144]{0:T(1024)} %bitcast.403, f32[6144,64]{1,0:T(8,128)} %copy.158, f32[]{:T(128)} %constant.142.clone.1), kind=kCustom, calls=%fused_computation.269 | custom fusion | flops 393216 | bytes 524800 | tf_op jit(solution)/shard_map/scatter-add | solution.py:147
  406.3 33.9 %scatter_fusion.5 = f32[64,2048]{0,1:T(8,128)S(1)} fusion(f32[64,2048]{0,1:T(8,128)S(1)} %scatter_custom_fusion.8, s32[6144]{0:T(1024)S(1)} %bitcast.387, f32[6144,64]{1,0:T(8,128)} %copy.159), kind=kCustom, calls=%fused_computation.25 | custom fusion | flops 393216 | bytes 4743168 | tf_op jit(solution)/shard_map/scatter-add | solution.py:149
  440.2 33.7 %scatter_custom_fusion = f32[3,2048]{0,1:T(8,128)S(1)} fusion(s32[6144]{0:T(1024)} %bitcast.404, f32[6144,3]{1,0:T(8,128)} %copy.148, f32[]{:T(128)} %constant.142.clone.1), kind=kCustom, calls=%fused_computation.271 | custom fusion | flops 18432 | bytes 25088 | tf_op jit(solution)/shard_map/scatter-add | solution.py:142
  473.9 33.9 %scatter_fusion = f32[3,2048]{0,1:T(8,128)S(1)} fusion(f32[3,2048]{0,1:T(8,128)S(1)} %scatter_custom_fusion, s32[6144]{0:T(1024)S(1)} %bitcast.388, f32[6144,3]{1,0:T(8,128)} %copy.149), kind=kCustom, calls=%fused_computation.17 | custom fusion | flops 18432 | bytes 245760 | tf_op jit(solution)/shard_map/scatter-add | solution.py:142
  507.8 157.6 %psum.7 = f32[]{:T(128)} all-reduce(f32[]{:T(128)S(6)} %add.371), channel_id=1, replica_groups=mesh['gx'=16,'gy'=2] {'gx','gy'}, use_global_device_ids=true, to_apply=%region_18.19 | all-reduce | flops 1 | bytes 8 | tf_op jit(solution)/shard_map/psum | solution.py:193
  672.0 11.9 %scatter_fusion.6 = f32[64,2048]{0,1:T(8,128)S(1)} fusion(f32[64,2048]{0,1:T(8,128)S(1)} %scatter_fusion.5, s32[2048]{0:T(1024)S(1)} %bitcast.393, f32[2048,64]{1,0:T(8,128)S(1)} %copy.160), kind=kCustom, calls=%fused_computation.26 | custom fusion | flops 131072 | bytes 1581056 | tf_op jit(solution)/shard_map/scatter-add | solution.py:167
  683.8 12.2 %scatter_fusion.7 = f32[64,2048]{0,1:T(8,128)S(1)} fusion(f32[64,2048]{0,1:T(8,128)S(1)} %scatter_fusion.6, s32[2048]{0:T(1024)S(1)} %bitcast.396, f32[2048,64]{1,0:T(8,128)} %copy.161), kind=kCustom, calls=%fused_computation.27 | custom fusion | flops 131072 | bytes 1581056 | tf_op jit(solution)/shard_map/scatter-add | solution.py:184
  696.1 12.2 %scatter_fusion.1 = f32[3,2048]{0,1:T(8,128)S(1)} fusion(f32[3,2048]{0,1:T(8,128)S(1)} %scatter_fusion, s32[2048]{0:T(1024)S(1)} %bitcast.394, f32[2048,3]{1,0:T(8,128)} %copy.150), kind=kCustom, calls=%fused_computation.18 | custom fusion | flops 6144 | bytes 81920 | tf_op jit(solution)/shard_map/scatter-add | solution.py:166
  708.3 12.2 %scatter_fusion.2 = f32[3,2048]{0,1:T(8,128)S(1)} fusion(f32[3,2048]{0,1:T(8,128)S(1)} %scatter_fusion.1, s32[2048]{0:T(1024)S(1)} %bitcast.397, f32[2048,3]{1,0:T(8,128)} %copy.151), kind=kCustom, calls=%fused_computation.19 | custom fusion | flops 6144 | bytes 81920 | tf_op jit(solution)/shard_map/scatter-add | solution.py:183
  733.3 9.7 %scatter_fusion.4 = f32[3,2048]{0,1:T(8,128)S(1)} fusion(f32[3,2048]{0,1:T(8,128)S(1)} %scatter_fusion.3, s32[1536]{0:T(1024)S(1)} %get-tuple-element.732, f32[1536,3]{1,0:T(8,128)} %copy.157), kind=kCustom, calls=%fused_computation.23 | custom fusion | flops 4608 | bytes 61440 | tf_op jit(solution)/shard_map/scatter-add | solution.py:191
  746.6 9.1 %scatter_fusion.8 = f32[64,2048]{0,1:T(8,128)S(1)} fusion(f32[64,2048]{0,1:T(8,128)S(1)} %scatter_fusion.7, s32[1536]{0:T(1024)S(1)} %get-tuple-element.733, f32[1536,64]{1,0:T(8,128)S(1)} %copy.164), kind=kCustom, calls=%fused_computation.29 | custom fusion | flops 98304 | bytes 1185792 | tf_op jit(solution)/shard_map/scatter-add | solution.py:192
  (294 shorter events, 225.8 us)
Async XLA Ops:
  0.6 10.4 %copy-start.11 = (bf16[64,2048]{1,0:T(8,128)(2,1)S(1)}, bf16[64,2048]{1,0:T(8,128)(2,1)}, u32[]{:S(2)}) copy-start(bf16[64,2048]{1,0:T(8,128)(2,1)} %param.24) | copy-start | bytes 786436
  5.5 154.5 %collective-permute-start = (f32[3,1536]{1,0:T(4,128)S(1)}, f32[3,1536]{1,0:T(4,128)S(1)}, u32[]{:S(2)}, u32[]{:S(2)}) collective-permute-start(f32[3,1536]{1,0:T(4,128)S(1)} %copy.121), channel_id=1, source_target_pairs={{0,30},{2,0},{4,2},{6,4},{8,6},{10,8},{12,10},{14,12},{16,14},{18,... | collective-permute-start | bytes 55304 | tf_op jit(solution)/shard_map/ppermute | solution.py:14
  15.3 10.2 %copy-start.19 = (s32[4,6144]{1,0:T(4,128)S(1)}, s32[4,6144]{1,0:T(4,128)}, u32[]{:S(2)}) copy-start(s32[4,6144]{1,0:T(4,128)} %param.26) | copy-start | bytes 294916
  15.3 11.0 %copy-start.21 = (s32[4,2048]{1,0:T(4,128)S(1)}, s32[4,2048]{1,0:T(4,128)}, u32[]{:S(2)}) copy-start(s32[4,2048]{1,0:T(4,128)} %param.27) | copy-start | bytes 98308
  15.3 11.0 %copy-start.22 = (s32[4,2048]{1,0:T(4,128)S(1)}, s32[4,2048]{1,0:T(4,128)}, u32[]{:S(2)}) copy-start(s32[4,2048]{1,0:T(4,128)} %param.28) | copy-start | bytes 98308
  15.3 163.6 %collective-permute-start.1 = (bf16[64,1536]{0,1:T(8,128)(2,1)}, bf16[64,1536]{0,1:T(8,128)(2,1)S(1)}, u32[]{:S(2)}, u32[]{:S(2)}) collective-permute-start(bf16[64,1536]{0,1:T(8,128)(2,1)} %bitcast.32), channel_id=1, source_target_pairs={{0,30},{2,0},{4,2},{6,4},{8,6},{10,8},{12,10},{14,12},{16,14},{18,... | collective-permute-start | bytes 589832 | tf_op jit(solution)/shard_map/ppermute | solution.py:14
  16.1 11.0 %copy-start.26 = (s32[1,3]{1,0:T(1,128)S(1)}, s32[1,3]{1,0:T(1,128)}, u32[]{:S(2)}) copy-start(s32[1,3]{1,0:T(1,128)} %param.29) | copy-start | bytes 40
  19.5 149.9 %collective-permute-start.2 = (f32[3,1536]{1,0:T(4,128)}, f32[3,1536]{1,0:T(4,128)S(1)}, u32[]{:S(2)}, u32[]{:S(2)}) collective-permute-start(f32[3,1536]{1,0:T(4,128)} %copy.135), channel_id=1, source_target_pairs={{0,1},{1,0},{2,3},{3,2},{4,5},{5,4},{6,7},{7,6},{8,9},{9,8},{10,11... | collective-permute-start | bytes 55304 | tf_op jit(solution)/shard_map/ppermute | solution.py:14
  25.0 178.5 %collective-permute-start.3 = (bf16[64,1536]{0,1:T(8,128)(2,1)}, bf16[64,1536]{0,1:T(8,128)(2,1)S(1)}, u32[]{:S(2)}, u32[]{:S(2)}) collective-permute-start(bf16[64,1536]{0,1:T(8,128)(2,1)} %bitcast.46), channel_id=1, source_target_pairs={{0,1},{1,0},{2,3},{3,2},{4,5},{5,4},{6,7},{7,6},{8,9},{9,8},{10,11... | collective-permute-start | bytes 589832 | tf_op jit(solution)/shard_map/ppermute | solution.py:14
  25.6 48.4 %copy-start.20 = (s32[6144,1]{0,1:T(1,128)}, s32[6144,1]{0,1:T(1,128)S(1)}, u32[]{:S(2)}) copy-start(s32[6144,1]{0,1:T(1,128)S(1)} %get-tuple-element.893) | copy-start | bytes 73732
  26.3 47.7 %copy-start.24 = (s32[2048,1]{0,1:T(1,128)}, s32[2048,1]{0,1:T(1,128)S(1)}, u32[]{:S(2)}) copy-start(s32[2048,1]{0,1:T(1,128)S(1)} %get-tuple-element.902) | copy-start | bytes 24580
  178.9 6.6 copy-start.8
  178.9 6.6 copy-start.9
  178.9 6.6 copy-start.10
  178.9 6.6 copy-start.18
  230.8 14.4 %copy-start.5 = (f32[64,2048]{1,0:T(8,128)}, f32[64,2048]{1,0:T(8,128)S(1)}, u32[]{:S(2)}) copy-start(f32[64,2048]{1,0:T(8,128)S(1)} %get-tuple-element.376) | copy-start | bytes 1572868
  230.8 14.4 %copy-start.14 = (f32[3,2048]{1,0:T(4,128)}, f32[3,2048]{1,0:T(4,128)S(1)}, u32[]{:S(2)}) copy-start(f32[3,2048]{1,0:T(4,128)S(1)} %get-tuple-element.370) | copy-start | bytes 73732
  230.9 14.4 %copy-start.16 = (f32[3,2048]{1,0:T(4,128)}, f32[3,2048]{1,0:T(4,128)S(1)}, u32[]{:S(2)}) copy-start(f32[3,2048]{1,0:T(4,128)S(1)} %get-tuple-element.372) | copy-start | bytes 73732
  245.3 498.8 %collective-permute-start.6 = (f32[64,1536]{1,0:T(8,128)}, f32[64,1536]{1,0:T(8,128)}, u32[]{:S(2)}, u32[]{:S(2)}) collective-permute-start(f32[64,1536]{1,0:T(8,128)} %copy.163), channel_id=1, source_target_pairs={{0,2},{2,4},{4,6},{6,8},{8,10},{10,12},{12,14},{14,16},{16,18},{18... | collective-permute-start | bytes 1179656 | tf_op jit(solution)/shard_map/ppermute | solution.py:14
  256.2 13.1 %copy-start.13 = (f32[3,2048]{1,0:T(4,128)S(1)}, f32[3,2048]{1,0:T(4,128)}, u32[]{:S(2)}) copy-start(f32[3,2048]{1,0:T(4,128)} %copy-done.12) | copy-start | bytes 73732
  269.3 39.4 %copy-start.17 = (f32[3,2048]{1,0:T(4,128)S(1)}, f32[3,2048]{1,0:T(4,128)}, u32[]{:S(2)}) copy-start(f32[3,2048]{1,0:T(4,128)} %copy-done.16) | copy-start | bytes 73732
  269.3 476.0 %collective-permute-start.7 = (f32[64,1536]{1,0:T(8,128)}, f32[64,1536]{1,0:T(8,128)}, u32[]{:S(2)}, u32[]{:S(2)}) collective-permute-start(f32[64,1536]{1,0:T(8,128)} %copy.166), channel_id=1, source_target_pairs={{0,1},{1,0},{2,3},{3,2},{4,5},{5,4},{6,7},{7,6},{8,9},{9,8},{10,11... | collective-permute-start | bytes 1179656 | tf_op jit(solution)/shard_map/ppermute | solution.py:14
  282.4 438.9 %collective-permute-start.4 = (f32[3,1536]{1,0:T(4,128)}, f32[3,1536]{1,0:T(4,128)}, u32[]{:S(2)}, u32[]{:S(2)}) collective-permute-start(f32[3,1536]{1,0:T(4,128)} %copy.153), channel_id=1, source_target_pairs={{0,2},{2,4},{4,6},{6,8},{8,10},{10,12},{12,14},{14,16},{16,18},{18... | collective-permute-start | bytes 55304 | tf_op jit(solution)/shard_map/ppermute | solution.py:14
  321.7 400.5 %collective-permute-start.5 = (f32[3,1536]{1,0:T(4,128)}, f32[3,1536]{1,0:T(4,128)}, u32[]{:S(2)}, u32[]{:S(2)}) collective-permute-start(f32[3,1536]{1,0:T(4,128)} %copy.156), channel_id=1, source_target_pairs={{0,1},{1,0},{2,3},{3,2},{4,5},{5,4},{6,7},{7,6},{8,9},{9,8},{10,11... | collective-permute-start | bytes 55304 | tf_op jit(solution)/shard_map/ppermute | solution.py:14
  (15 other events, 61.5 us)
where the time goes:
time: 780 us; the launch traced here: 767 us
  other arithmetic  287 us (37%)
  local copies, waits for them, and re-layouts  214 us (27%)
  blocking collectives  158 us (20%)
  matrix products  51.4 us (7%)
  starting transfers between devices  45.8 us (6%)
    psum x1, blocking collectives, on_device(): total = lax.psum(energy_loc + energy_x + energy_y, ('gx', 'gy'))  158 us
    scatter-add x2, other arithmetic, on_device(): jnp.zeros((3, atoms), jnp.float32).at[:, source].add(grads[0]).at[:, target]  67.6 us
    scatter-add x2, other arithmetic, on_device(): grad_feat = jnp.zeros((width, atoms), jnp.float32).at[:, source].add(grad...  67.6 us
    ppermute x8, starting transfers between devices, shifted(): lax.ppermute(array, axis, [(i, (i + by) % length) for i in range(length)])  45.8 us
    while x16, local copies, waits for them, and re-layouts, run_edges(): lax.fori_loop(0, filled, visit_live, (jnp.zeros((), jnp.float32), start_g...  27.8 us
    dot_general x14, matrix products, pair_energy(): jnp.dot(w_hidden.T, hidden, preferred_element_type=jnp.float32)  22.1 us
    gather x1, local copies, waits for them, and re-layouts, on_device(): features[:, source]  22.1 us
    gather x1, local copies, waits for them, and re-layouts, on_device(): features[:, target]  22 us
  transfers between devices with their start and end apart: 8, of which 0 were waited for; matrix products, arithmetic and copies ran while one was open for 64% of the time, Pallas kernels for 0%

commit v1 on v0

--- a/solution.py
+++ b/solution.py
@@ -190,7 +190,9 @@
     back_pos_y, back_feat_y = shifted((lent_pos_y, lent_feat_y), "gy", 1)
     grad_pos = grad_pos.at[:, list_x].add(back_pos_x).at[:, list_y].add(back_pos_y)
     grad_feat = grad_feat.at[:, list_x].add(back_feat_x).at[:, list_y].add(back_feat_y)
-    total = lax.psum(energy_loc + energy_x + energy_y, ("gx", "gy"))
+    total = energy_loc + energy_x + energy_y
+    for mesh_axis in ("gy", "gx"):
+        total = lax.psum(total, mesh_axis)
     atoms_all = atoms * lax.axis_size("gx") * lax.axis_size("gy")
     energy = (total / atoms_all).reshape(1)
     return (energy, -grad_pos, grad_feat)

time: 780 us -> 773 us (level)
  blocking collectives: 158 us -> 150 us
    psum x1 -> x2, blocking collectives: 158 us -> 150 us  [on_device(): total = lax.psum(total, mesh_axis)]
where the time goes in v1:
time: 773 us; the launch traced here: 760 us
  other arithmetic  288 us (37%)
  local copies, waits for them, and re-layouts  214 us (28%)
  blocking collectives  150 us (19%)
  matrix products  51.4 us (7%)
  starting transfers between devices  45.8 us (6%)
    psum x2, blocking collectives, on_device(): total = lax.psum(total, mesh_axis)  150 us
    scatter-add x2, other arithmetic, on_device(): grad_feat = jnp.zeros((width, atoms), jnp.float32).at[:, source].add(grad...  67.6 us
    scatter-add x2, other arithmetic, on_device(): jnp.zeros((3, atoms), jnp.float32).at[:, source].add(grads[0]).at[:, target]  67.6 us
    ppermute x8, starting transfers between devices, shifted(): lax.ppermute(array, axis, [(i, (i + by) % length) for i in range(length)])  45.8 us
    while x16, local copies, waits for them, and re-layouts, run_edges(): lax.fori_loop(0, filled, visit_live, (jnp.zeros((), jnp.float32), start_g...  27.8 us
    dot_general x14, matrix products, pair_energy(): jnp.dot(w_hidden.T, hidden, preferred_element_type=jnp.float32)  22.1 us
    gather x1, local copies, waits for them, and re-layouts, on_device(): features[:, source]  22.1 us
    gather x1, local copies, waits for them, and re-layouts, on_device(): features[:, target]  22 us
  transfers between devices with their start and end apart: 8, of which 0 were waited for; matrix products, arithmetic and copies ran while one was open for 64% of the time, Pallas kernels for 0%

profile of v1, /device:TPU:0, one launch (start us, length us, event | category | flops | bytes accessed | tf_op | source)
XLA Modules:
  0.0 760.4 jit_solution(16097306824922658178)
XLA Ops:
  31.0 20.9 %gather_fusion.1 = f32[6144,3]{1,0:T(8,128)} fusion(f32[3,2048]{0,1:T(8,128)S(1)} %copy.112, s32[6144]{0:T(1024)S(1)} %broadcast_clamp_fusion), kind=kCustom, calls=%fused_computation.1 | custom fusion | bytes 172032 | tf_op jit(solution)/shard_map/gather | solution.py:130
  51.9 22.1 %gather_fusion.2 = bf16[6144,64]{1,0:T(8,128)(2,1)} fusion(bf16[64,2048]{0,1:T(8,128)(2,1)S(1)} %copy.114, s32[6144]{0:T(1024)S(1)} %broadcast_clamp_fusion), kind=kCustom, calls=%fused_computation.2 | custom fusion | bytes 1597440 | tf_op jit(solution)/shard_map/gather | solution.py:131
  74.0 20.9 %gather_fusion = f32[6144,3]{1,0:T(8,128)} fusion(f32[3,2048]{0,1:T(8,128)S(1)} %copy.112, s32[6144]{0:T(1024)S(1)} %broadcast_clamp_fusion.1), kind=kCustom, calls=%fused_computation | custom fusion | bytes 172032 | tf_op jit(solution)/shard_map/gather | solution.py:132
  94.9 22.0 %gather_fusion.3 = bf16[6144,64]{1,0:T(8,128)(2,1)} fusion(bf16[64,2048]{0,1:T(8,128)(2,1)S(1)} %copy.114, s32[6144]{0:T(1024)S(1)} %broadcast_clamp_fusion.1), kind=kCustom, calls=%fused_computation.3 | custom fusion | bytes 1597440 | tf_op jit(solution)/shard_map/gather | solution.py:133
  185.6 17.9 %while.57 = (s32[]{:T(128)}, f32[]{:T(128)}, f32[3,2048]{1,0:T(4,128)S(1)}, f32[64,2048]{1,0:T(8,128)S(1)}, f32[3,2048]{1,0:T(4,128)S(1)}, /*index=5*/f32[64,204...) while((s32[]{:T(128)}, f32[]{:T(128)}, ...), condition=%wide.region_11.12_spmd.clone, body=%wide.region_6.11_spmd.sunk.clone.sunk | while | flops 246594080 | bytes 9612223 | solution.py:89
  210.1 20.8 %while.58 = (s32[]{:T(128)}, f32[]{:T(128)}, f32[3,2048]{1,0:T(4,128)S(1)}, f32[64,2048]{1,0:T(8,128)S(1)}, f32[3,2048]{1,0:T(4,128)S(1)}, /*index=5*/f32[64,204...) while((s32[]{:T(128)}, f32[]{:T(128)}, ...), condition=%wide.region_17.18_spmd.clone, body=%wide.region_12.17_spmd.sunk.clone.sunk | while | flops 246594080 | bytes 9743323 | solution.py:89
  232.2 12.0 %scatter_custom_fusion.12 = f32[64,1536]{0,1:T(8,128)S(1)} fusion(s32[2048]{0:T(1024)} %bitcast.415, f32[2048,64]{1,0:T(8,128)} %copy.162, f32[]{:T(128)} %constant.142.clone.1), kind=kCustom, calls=%fused_computation.275 | custom fusion | flops 131072 | bytes 393728 | tf_op jit(solution)/shard_map/scatter-add | solution.py:186
  245.3 10.9 %collective-permute-start.6 = (f32[64,1536]{1,0:T(8,128)}, f32[64,1536]{1,0:T(8,128)}, u32[]{:S(2)}, u32[]{:S(2)}) collective-permute-start(f32[64,1536]{1,0:T(8,128)} %copy.163), channel_id=1, source_target_pairs={{0,2},{2,4},{4,6},{6,8},{8,10},{10,12},{12,14},{14,16},{16,18},{18... | collective-permute-start | bytes 1179656 | tf_op jit(solution)/shard_map/ppermute | solution.py:14
  256.5 11.8 %scatter_custom_fusion.14 = f32[64,1536]{0,1:T(8,128)S(1)} fusion(s32[2048]{0:T(1024)} %bitcast.412, f32[2048,64]{1,0:T(8,128)S(1)} %copy.165, f32[]{:T(128)} %constant.142.clone.1), kind=kCustom, calls=%fused_computation.273 | custom fusion | flops 131072 | bytes 393728 | tf_op jit(solution)/shard_map/scatter-add | solution.py:189
  269.7 11.8 %scatter_custom_fusion.4 = f32[3,1536]{0,1:T(8,128)S(1)} fusion(s32[2048]{0:T(1024)} %bitcast.416, f32[2048,3]{1,0:T(8,128)S(1)} %copy.152, f32[]{:T(128)} %constant.142.clone.1), kind=kCustom, calls=%fused_computation.279 | custom fusion | flops 6144 | bytes 18944 | tf_op jit(solution)/shard_map/scatter-add | solution.py:185
  282.4 26.4 %collective-permute-start.4 = (f32[3,1536]{1,0:T(4,128)}, f32[3,1536]{1,0:T(4,128)}, u32[]{:S(2)}, u32[]{:S(2)}) collective-permute-start(f32[3,1536]{1,0:T(4,128)} %copy.153), channel_id=1, source_target_pairs={{0,2},{2,4},{4,6},{6,8},{8,10},{10,12},{12,14},{14,16},{16,18},{18... | collective-permute-start | bytes 55304 | tf_op jit(solution)/shard_map/ppermute | solution.py:14
  309.1 11.8 %scatter_custom_fusion.6 = f32[3,1536]{0,1:T(8,128)S(1)} fusion(s32[2048]{0:T(1024)} %bitcast.413, f32[2048,3]{1,0:T(8,128)S(1)} %copy.155, f32[]{:T(128)} %constant.142.clone.1), kind=kCustom, calls=%fused_computation.277 | custom fusion | flops 6144 | bytes 18944 | tf_op jit(solution)/shard_map/scatter-add | solution.py:188
  323.5 40.1 %while.56 = (s32[]{:T(128)}, f32[]{:T(128)}, f32[3,6144]{1,0:T(4,128)S(1)}, f32[64,6144]{1,0:T(8,128)S(1)}, f32[3,6144]{1,0:T(4,128)S(1)}, /*index=5*/f32[64,614...) while((s32[]{:T(128)}, f32[]{:T(128)}, ...), condition=%wide.region_5.6_spmd, body=%wide.region_0.5_spmd.sunk | while | flops 246594080 | bytes 9610155 | solution.py:89
  372.5 33.7 %scatter_custom_fusion.8 = f32[64,2048]{0,1:T(8,128)S(1)} fusion(s32[6144]{0:T(1024)} %bitcast.403, f32[6144,64]{1,0:T(8,128)} %copy.158, f32[]{:T(128)} %constant.142.clone.1), kind=kCustom, calls=%fused_computation.269 | custom fusion | flops 393216 | bytes 524800 | tf_op jit(solution)/shard_map/scatter-add | solution.py:147
  406.3 33.9 %scatter_fusion.5 = f32[64,2048]{0,1:T(8,128)S(1)} fusion(f32[64,2048]{0,1:T(8,128)S(1)} %scatter_custom_fusion.8, s32[6144]{0:T(1024)S(1)} %bitcast.387, f32[6144,64]{1,0:T(8,128)} %copy.159), kind=kCustom, calls=%fused_computation.25 | custom fusion | flops 393216 | bytes 4743168 | tf_op jit(solution)/shard_map/scatter-add | solution.py:149
  440.2 33.7 %scatter_custom_fusion = f32[3,2048]{0,1:T(8,128)S(1)} fusion(s32[6144]{0:T(1024)} %bitcast.404, f32[6144,3]{1,0:T(8,128)} %copy.148, f32[]{:T(128)} %constant.142.clone.1), kind=kCustom, calls=%fused_computation.271 | custom fusion | flops 18432 | bytes 25088 | tf_op jit(solution)/shard_map/scatter-add | solution.py:142
  473.9 45.1 %psum.14 = f32[]{:T(128)} all-reduce(f32[]{:T(128)S(6)} %add.373), channel_id=1, replica_groups=mesh['gx'=16,'gy'=2] {'gy'}, use_global_device_ids=true, to_apply=%region_18.19 | all-reduce | flops 1 | bytes 8 | tf_op jit(solution)/shard_map/psum | solution.py:195
  519.0 33.9 %scatter_fusion = f32[3,2048]{0,1:T(8,128)S(1)} fusion(f32[3,2048]{0,1:T(8,128)S(1)} %scatter_custom_fusion, s32[6144]{0:T(1024)S(1)} %bitcast.388, f32[6144,3]{1,0:T(8,128)} %copy.149), kind=kCustom, calls=%fused_computation.17 | custom fusion | flops 18432 | bytes 245760 | tf_op jit(solution)/shard_map/scatter-add | solution.py:142
  552.9 105.2 %psum.15 = f32[]{:T(128)} all-reduce(f32[]{:T(128)} %psum.14), channel_id=1, replica_groups=mesh['gx'=16,'gy'=2] {'gx'}, use_global_device_ids=true, to_apply=%region_19.20 | all-reduce | flops 1 | bytes 8 | tf_op jit(solution)/shard_map/psum | solution.py:195
  664.6 12.3 %scatter_fusion.6 = f32[64,2048]{0,1:T(8,128)S(1)} fusion(f32[64,2048]{0,1:T(8,128)S(1)} %scatter_fusion.5, s32[2048]{0:T(1024)S(1)} %bitcast.393, f32[2048,64]{1,0:T(8,128)S(1)} %copy.160), kind=kCustom, calls=%fused_computation.26 | custom fusion | flops 131072 | bytes 1581056 | tf_op jit(solution)/shard_map/scatter-add | solution.py:167
  676.9 12.2 %scatter_fusion.7 = f32[64,2048]{0,1:T(8,128)S(1)} fusion(f32[64,2048]{0,1:T(8,128)S(1)} %scatter_fusion.6, s32[2048]{0:T(1024)S(1)} %bitcast.396, f32[2048,64]{1,0:T(8,128)} %copy.161), kind=kCustom, calls=%fused_computation.27 | custom fusion | flops 131072 | bytes 1581056 | tf_op jit(solution)/shard_map/scatter-add | solution.py:184
  689.1 12.2 %scatter_fusion.1 = f32[3,2048]{0,1:T(8,128)S(1)} fusion(f32[3,2048]{0,1:T(8,128)S(1)} %scatter_fusion, s32[2048]{0:T(1024)S(1)} %bitcast.394, f32[2048,3]{1,0:T(8,128)} %copy.150), kind=kCustom, calls=%fused_computation.18 | custom fusion | flops 6144 | bytes 81920 | tf_op jit(solution)/shard_map/scatter-add | solution.py:166
  701.4 12.2 %scatter_fusion.2 = f32[3,2048]{0,1:T(8,128)S(1)} fusion(f32[3,2048]{0,1:T(8,128)S(1)} %scatter_fusion.1, s32[2048]{0:T(1024)S(1)} %bitcast.397, f32[2048,3]{1,0:T(8,128)} %copy.151), kind=kCustom, calls=%fused_computation.19 | custom fusion | flops 6144 | bytes 81920 | tf_op jit(solution)/shard_map/scatter-add | solution.py:183
  726.4 9.5 %scatter_fusion.4 = f32[3,2048]{0,1:T(8,128)S(1)} fusion(f32[3,2048]{0,1:T(8,128)S(1)} %scatter_fusion.3, s32[1536]{0:T(1024)S(1)} %get-tuple-element.732, f32[1536,3]{1,0:T(8,128)} %copy.157), kind=kCustom, calls=%fused_computation.23 | custom fusion | flops 4608 | bytes 61440 | tf_op jit(solution)/shard_map/scatter-add | solution.py:191
  (295 shorter events, 235.1 us)
Async XLA Ops:
  0.6 10.4 %copy-start.11 = (bf16[64,2048]{1,0:T(8,128)(2,1)S(1)}, bf16[64,2048]{1,0:T(8,128)(2,1)}, u32[]{:S(2)}) copy-start(bf16[64,2048]{1,0:T(8,128)(2,1)} %param.24) | copy-start | bytes 786436
  5.5 154.5 %collective-permute-start = (f32[3,1536]{1,0:T(4,128)S(1)}, f32[3,1536]{1,0:T(4,128)S(1)}, u32[]{:S(2)}, u32[]{:S(2)}) collective-permute-start(f32[3,1536]{1,0:T(4,128)S(1)} %copy.121), channel_id=1, source_target_pairs={{0,30},{2,0},{4,2},{6,4},{8,6},{10,8},{12,10},{14,12},{16,14},{18,... | collective-permute-start | bytes 55304 | tf_op jit(solution)/shard_map/ppermute | solution.py:14
  15.3 10.2 %copy-start.19 = (s32[4,6144]{1,0:T(4,128)S(1)}, s32[4,6144]{1,0:T(4,128)}, u32[]{:S(2)}) copy-start(s32[4,6144]{1,0:T(4,128)} %param.26) | copy-start | bytes 294916
  15.3 11.0 %copy-start.21 = (s32[4,2048]{1,0:T(4,128)S(1)}, s32[4,2048]{1,0:T(4,128)}, u32[]{:S(2)}) copy-start(s32[4,2048]{1,0:T(4,128)} %param.27) | copy-start | bytes 98308
  15.3 11.0 %copy-start.22 = (s32[4,2048]{1,0:T(4,128)S(1)}, s32[4,2048]{1,0:T(4,128)}, u32[]{:S(2)}) copy-start(s32[4,2048]{1,0:T(4,128)} %param.28) | copy-start | bytes 98308
  15.3 163.6 %collective-permute-start.1 = (bf16[64,1536]{0,1:T(8,128)(2,1)}, bf16[64,1536]{0,1:T(8,128)(2,1)S(1)}, u32[]{:S(2)}, u32[]{:S(2)}) collective-permute-start(bf16[64,1536]{0,1:T(8,128)(2,1)} %bitcast.32), channel_id=1, source_target_pairs={{0,30},{2,0},{4,2},{6,4},{8,6},{10,8},{12,10},{14,12},{16,14},{18,... | collective-permute-start | bytes 589832 | tf_op jit(solution)/shard_map/ppermute | solution.py:14
  16.1 11.0 %copy-start.26 = (s32[1,3]{1,0:T(1,128)S(1)}, s32[1,3]{1,0:T(1,128)}, u32[]{:S(2)}) copy-start(s32[1,3]{1,0:T(1,128)} %param.29) | copy-start | bytes 40
  19.5 149.9 %collective-permute-start.2 = (f32[3,1536]{1,0:T(4,128)}, f32[3,1536]{1,0:T(4,128)S(1)}, u32[]{:S(2)}, u32[]{:S(2)}) collective-permute-start(f32[3,1536]{1,0:T(4,128)} %copy.135), channel_id=1, source_target_pairs={{0,1},{1,0},{2,3},{3,2},{4,5},{5,4},{6,7},{7,6},{8,9},{9,8},{10,11... | collective-permute-start | bytes 55304 | tf_op jit(solution)/shard_map/ppermute | solution.py:14
  25.0 178.5 %collective-permute-start.3 = (bf16[64,1536]{0,1:T(8,128)(2,1)}, bf16[64,1536]{0,1:T(8,128)(2,1)S(1)}, u32[]{:S(2)}, u32[]{:S(2)}) collective-permute-start(bf16[64,1536]{0,1:T(8,128)(2,1)} %bitcast.46), channel_id=1, source_target_pairs={{0,1},{1,0},{2,3},{3,2},{4,5},{5,4},{6,7},{7,6},{8,9},{9,8},{10,11... | collective-permute-start | bytes 589832 | tf_op jit(solution)/shard_map/ppermute | solution.py:14
  25.6 48.4 %copy-start.20 = (s32[6144,1]{0,1:T(1,128)}, s32[6144,1]{0,1:T(1,128)S(1)}, u32[]{:S(2)}) copy-start(s32[6144,1]{0,1:T(1,128)S(1)} %get-tuple-element.893) | copy-start | bytes 73732
  26.3 47.7 %copy-start.24 = (s32[2048,1]{0,1:T(1,128)}, s32[2048,1]{0,1:T(1,128)S(1)}, u32[]{:S(2)}) copy-start(s32[2048,1]{0,1:T(1,128)S(1)} %get-tuple-element.902) | copy-start | bytes 24580
  178.9 6.6 copy-start.8
  178.9 6.6 copy-start.9
  178.9 6.6 copy-start.10
  178.9 6.6 copy-start.18
  230.8 14.4 %copy-start.5 = (f32[64,2048]{1,0:T(8,128)}, f32[64,2048]{1,0:T(8,128)S(1)}, u32[]{:S(2)}) copy-start(f32[64,2048]{1,0:T(8,128)S(1)} %get-tuple-element.376) | copy-start | bytes 1572868
  230.8 14.4 %copy-start.14 = (f32[3,2048]{1,0:T(4,128)}, f32[3,2048]{1,0:T(4,128)S(1)}, u32[]{:S(2)}) copy-start(f32[3,2048]{1,0:T(4,128)S(1)} %get-tuple-element.370) | copy-start | bytes 73732
  230.9 14.4 %copy-start.16 = (f32[3,2048]{1,0:T(4,128)}, f32[3,2048]{1,0:T(4,128)S(1)}, u32[]{:S(2)}) copy-start(f32[3,2048]{1,0:T(4,128)S(1)} %get-tuple-element.372) | copy-start | bytes 73732
  245.3 491.7 %collective-permute-start.6 = (f32[64,1536]{1,0:T(8,128)}, f32[64,1536]{1,0:T(8,128)}, u32[]{:S(2)}, u32[]{:S(2)}) collective-permute-start(f32[64,1536]{1,0:T(8,128)} %copy.163), channel_id=1, source_target_pairs={{0,2},{2,4},{4,6},{6,8},{8,10},{10,12},{12,14},{14,16},{16,18},{18... | collective-permute-start | bytes 1179656 | tf_op jit(solution)/shard_map/ppermute | solution.py:14
  256.2 13.1 %copy-start.13 = (f32[3,2048]{1,0:T(4,128)S(1)}, f32[3,2048]{1,0:T(4,128)}, u32[]{:S(2)}) copy-start(f32[3,2048]{1,0:T(4,128)} %copy-done.12) | copy-start | bytes 73732
  269.3 39.4 %copy-start.17 = (f32[3,2048]{1,0:T(4,128)S(1)}, f32[3,2048]{1,0:T(4,128)}, u32[]{:S(2)}) copy-start(f32[3,2048]{1,0:T(4,128)} %copy-done.16) | copy-start | bytes 73732
  269.3 468.9 %collective-permute-start.7 = (f32[64,1536]{1,0:T(8,128)}, f32[64,1536]{1,0:T(8,128)}, u32[]{:S(2)}, u32[]{:S(2)}) collective-permute-start(f32[64,1536]{1,0:T(8,128)} %copy.166), channel_id=1, source_target_pairs={{0,1},{1,0},{2,3},{3,2},{4,5},{5,4},{6,7},{7,6},{8,9},{9,8},{10,11... | collective-permute-start | bytes 1179656 | tf_op jit(solution)/shard_map/ppermute | solution.py:14
  282.4 431.9 %collective-permute-start.4 = (f32[3,1536]{1,0:T(4,128)}, f32[3,1536]{1,0:T(4,128)}, u32[]{:S(2)}, u32[]{:S(2)}) collective-permute-start(f32[3,1536]{1,0:T(4,128)} %copy.153), channel_id=1, source_target_pairs={{0,2},{2,4},{4,6},{6,8},{8,10},{10,12},{12,14},{14,16},{16,18},{18... | collective-permute-start | bytes 55304 | tf_op jit(solution)/shard_map/ppermute | solution.py:14
  321.7 393.6 %collective-permute-start.5 = (f32[3,1536]{1,0:T(4,128)}, f32[3,1536]{1,0:T(4,128)}, u32[]{:S(2)}, u32[]{:S(2)}) collective-permute-start(f32[3,1536]{1,0:T(4,128)} %copy.156), channel_id=1, source_target_pairs={{0,1},{1,0},{2,3},{3,2},{4,5},{5,4},{6,7},{7,6},{8,9},{9,8},{10,11... | collective-permute-start | bytes 55304 | tf_op jit(solution)/shard_map/ppermute | solution.py:14
  (15 other events, 61.5 us)
